TPU v7x, 256 devices: a whole 4x4x8 slice. The times are simulated.
256 devices in a mesh: inner: 16 (over x, y), outer: 16 (over z, core).
Axes of the slice: x: 4, y: 4, z: 8, core: 2. Of those that a mesh axis runs over, the one named last changes fastest.
Arguments:
- jac: float32 [4096, 256, 256], P(('outer', 'inner')), may hold values from -0.5 to 1
- obs: float32 [4096, 256], P(('outer', 'inner')), may hold values from -6 to 6
- gain_filter: float32 [256], replicated, may hold values from 0 to 0.1
- gain_smooth: float32 [256, 256], replicated, may hold values from -0.5 to 1
- init_mean: float32 [256], replicated, may hold values from -6 to 6
Outputs:
- filtered: float32 [4096, 256], P(('outer', 'inner'))
- smoothed: float32 [4096, 256], P(('outer', 'inner'))
All inputs are finite; a program needn't handle non-finite values.
Results may differ from a plain program's by a relative error of at most 0.0003.
Values sent between devices are 32-bit elements; how exact they have to be, the bound alone decides.
No kernel may reach another device: no remote copies, remote signals or barrier semaphores. Data moves between devices by JAX's collectives and lax.ppermute only.
A program may use at most 64 MiB of HBM per device.

v0:
```python
import jax
import jax.numpy as jnp
from jax import lax
from jax.sharding import PartitionSpec as P

HIGHEST = lax.Precision.HIGHEST


def entering(part, axis, combine, identity, reverse):
    count = lax.axis_size(axis)
    place = lax.axis_index(axis)
    ahead = count - 1 - place if reverse else place
    gathered = lax.all_gather(part, axis)
    state = jnp.zeros_like(part) + jnp.asarray(identity, part.dtype)

    def one(turn, state):
        source = count - 1 - turn if reverse else turn
        return combine(state, lax.dynamic_index_in_dim(gathered, source, 0, False))

    return lax.fori_loop(0, ahead, one, state)


def last_row(state_width):
    return (jnp.arange(state_width + 1) == state_width).astype(jnp.float32)[:, None]


def identity_map(state_width):
    return jnp.concatenate(
        [jnp.eye(state_width, dtype=jnp.float32), jnp.zeros((1, state_width), jnp.float32)], 0
    )


def compose(earlier, later):
    state_width = later.shape[1]
    product = jnp.dot(earlier, later[:state_width], precision=HIGHEST)
    return product + last_row(state_width) * later[state_width][None, :]


def advance(packed, state):
    state_width = packed.shape[1]
    return jnp.dot(state, packed[:state_width], precision=HIGHEST) + packed[state_width]


def raise_power(factor, count):
    result = jnp.eye(factor.shape[0], dtype=jnp.float32)
    square = factor
    while count > 0:
        if count % 2 == 1:
            result = jnp.dot(result, square, precision=HIGHEST)
        count = count // 2
        if count > 0:
            square = jnp.dot(square, square, precision=HIGHEST)
    return result


def incoming_state(own_map, boundary, reverse):
    state_width = own_map.shape[1]
    identity = identity_map(state_width)
    inner_count = lax.axis_size("inner")
    inner_here = lax.axis_index("inner")
    gathered = lax.all_gather(own_map[None], "inner", axis=0, tiled=True)

    def absorb(running, inputs):
        before, group_total = running
        segment, position = inputs
        group_total = compose(group_total, segment)
        if reverse:
            taken = position > inner_here
        else:
            taken = position < inner_here
        before = jnp.where(taken, group_total, before)
        return ((before, group_total), None)

    (seg_before, group_total), _ = lax.scan(
        absorb,
        (identity, identity),
        (gathered, jnp.arange(inner_count, dtype=jnp.int32)),
        reverse=reverse,
    )
    group_before = entering(group_total, "outer", compose, identity, reverse)
    group_state = advance(group_before, boundary)
    return advance(seg_before, group_state)


def shards(jac, obs, gain_filter, gain_smooth, init_mean):
    state_width = jac.shape[1]
    step_count = jac.shape[0]
    retain = 1.0 - gain_filter
    bottom = last_row(state_width)

    def compose_forward(packed, inputs):
        step_matrix, measured = inputs
        moved = (
            lax.dot_general(packed, step_matrix, (((1,), (1,)), ((), ())), precision=HIGHEST)
            * retain[None, :]
        )
        return (moved + bottom * (gain_filter * measured)[None, :], None)

    forward_map, _ = lax.scan(compose_forward, identity_map(state_width), (jac, obs))
    start_state = incoming_state(forward_map, init_mean, False)

    def forward(state, inputs):
        step_matrix, measured = inputs
        predicted = jnp.dot(step_matrix, state, precision=HIGHEST)
        updated = predicted + gain_filter * (measured - predicted)
        return (updated, (predicted, updated))

    _, (predicted_all, filtered_all) = lax.scan(forward, start_state, (jac, obs))
    correction = filtered_all - predicted_all

    def backward(state, term):
        renewed = jnp.dot(gain_smooth, state, precision=HIGHEST) + term
        return (renewed, renewed)

    zero_state = jnp.zeros((state_width,), jnp.float32)
    offset_sum, _ = lax.scan(backward, zero_state, correction, reverse=True)
    step_power = raise_power(gain_smooth.T, step_count)
    backward_map = jnp.concatenate([step_power, offset_sum[None]], 0)
    after_state = incoming_state(backward_map, zero_state, True)
    _, back_states = lax.scan(backward, after_state, correction, reverse=True)
    return (filtered_all, predicted_all + back_states)


def solution(mesh):
    return jax.shard_map(
        shards,
        mesh=mesh,
        in_specs=(P(("outer", "inner"), None, None), P(("outer", "inner"), None), P(), P(), P()),
        out_specs=(P(("outer", "inner"), None), P(("outer", "inner"), None)),
        check_vma=False,
    )
```

profile of v0, /device:TPU:2, one launch (start us, length us, event | category | flops | bytes accessed | tf_op | source)
XLA Modules:
  0.0 473.1 jit_solution(15027441515699616519)
XLA Ops:
  8.0 34.7 %while.112 = (s32[]{:T(128)}, f32[257,256]{1,0:T(8,128)S(1)}, f32[16,256,256]{2,1,0:T(8,128)}, f32[256]{0:T(256)S(1)}, f32[256]{0:T(256)}, /*index=5*/f32[16,256]{1,0:T(8,128)}, s32[]{:T(128)}) while((s32[]{:T(128)}, f32[257,256]{1,0:T(8,128)S(1)}, f32[16,256,256]{2,1,0:T(8,128)}, f32[256]{0:T(256)S(1)}, f32[256]{0:T(256)}, ...), condition=%wide.region_1.2_spmd.clone, body=%wide.region_0.1_spmd.clone.sunk | while | flops 202311168 | bytes 1322585 | solution.py:99
  43.5 60.2 %all-gather.13.cloned.1.call-done = f32[16,257,256]{2,1,0:T(8,128)} async-done(((f32[1,257,256]{2,1,0:T(8,128)}), f32[16,257,256]{2,1,0:T(8,128)}) %all-gather.13.cloned.1.call-update) | async-done | bytes 4210704 | tf_op jit(solution)/shard_map/all_gather | solution.py:61
  103.8 55.9 %while.106 = (s32[]{:T(128)}, f32[257,256]{1,0:T(8,128)S(1)}, f32[257,256]{1,0:T(8,128)S(1)}, s32[16]{0:T(128)S(1)}, s32[]{:T(128)}, /*index=5*/f32[16,257,256]{2,1,0:T(8,128)}, s32[]{:T(128)}, s32[]{:T(128)}, s32[]{}) while((s32[]{:T(128)}, f32[257,256]{1,0:T(8,128)S(1)}, f32[257,256]{1,0:T(8,128)S(1)}, s32[16]{0:T(128)S(1)}, s32[]{:T(128)}, ...), condition=%wide.region_3.4_spmd, body=%wide.region_2.3_spmd.sunk | while | flops 202310912 | bytes 1846927 | solution.py:74
  105.8 1.5 broadcast_select_fusion.6
  109.3 1.5 broadcast_select_fusion.6
  112.8 1.5 broadcast_select_fusion.6
  116.2 1.5 broadcast_select_fusion.6
  119.7 1.5 broadcast_select_fusion.6
  123.2 1.5 broadcast_select_fusion.6
  126.7 1.5 broadcast_select_fusion.6
  130.2 1.5 broadcast_select_fusion.6
  133.7 1.5 broadcast_select_fusion.6
  137.2 1.5 broadcast_select_fusion.6
  140.7 1.5 broadcast_select_fusion.6
  144.2 1.5 broadcast_select_fusion.6
  147.7 1.5 broadcast_select_fusion.6
  151.2 1.5 broadcast_select_fusion.6
  158.2 1.5 broadcast_select_fusion.6
  162.6 40.0 %all-gather.15.cloned.1.call-done = f32[16,257,256]{2,1,0:T(8,128)} async-done(((f32[1,257,256]{2,1,0:T(8,128)}), f32[16,257,256]{2,1,0:T(8,128)}) %all-gather.15.cloned.1.call-update) | async-done | bytes 4210704 | tf_op jit(solution)/shard_map/all_gather | solution.py:13
  203.1 33.3 %while.108 = (s32[]{:T(128)}, f32[256]{0:T(256)S(1)}, f32[16,256]{1,0:T(8,128)S(1)}, f32[16,256]{1,0:T(8,128)S(1)}, f32[16,256,256]{2,1,0:T(8,128)}, /*index=5*/...) while((s32[]{:T(128)}, f32[256]{0:T(256)S(1)}, f32[16,256]{1,0:T(8,128)S(1)}, ...), condition=%wide.region_7.8_spmd, body=%wide.region_6.7_spmd.sunk | while | flops 787202 | bytes 275049 | solution.py:108
  236.4 6.1 %while.113 = (s32[]{:T(128)}, f32[256]{0:T(256)S(1)}, f32[256,256]{1,0:T(8,128)S(1)}, f32[16,256]{1,0:T(8,128)S(1)}, s32[]{:T(128)}, /*index=5*/s32[]{:T(128)}, s32[]{:T(128)}) while((s32[]{:T(128)}, f32[256]{0:T(256)S(1)}, f32[256,256]{1,0:T(8,128)S(1)}, f32[16,256]{1,0:T(8,128)S(1)}, s32[]{:T(128)}, /*index=5*/s32[]{:T(128)}, ...), condition=%wide.region_9.10_spmd.clone, body=%wide.region_8.9_spmd.clone.sunk | while | flops 786948 | bytes 271463 | solution.py:116
  243.4 86.6 %all-gather.17.cloned.1.call-done = f32[16,257,256]{2,1,0:T(8,128)} async-done(((f32[1,257,256]{2,1,0:T(8,128)}), f32[16,257,256]{2,1,0:T(8,128)}) %all-gather.17.cloned.1.call-update) | async-done | bytes 4210704 | tf_op jit(solution)/shard_map/all_gather | solution.py:61
  330.0 54.4 %while.109 = (s32[]{:T(128)}, f32[257,256]{1,0:T(8,128)S(1)}, f32[257,256]{1,0:T(8,128)S(1)}, s32[16]{0:T(128)S(1)}, s32[]{:T(128)}, /*index=5*/f32[16,257,256]{2,1,0:T(8,128)}, s32[]{:T(128)}, s32[]{:T(128)}, s32[]{:T(128)}, s32[]{}) while((s32[]{:T(128)}, f32[257,256]{1,0:T(8,128)S(1)}, f32[257,256]{1,0:T(8,128)S(1)}, s32[16]{0:T(128)S(1)}, ...), condition=%wide.region_11.12_spmd, body=%wide.region_10.11_spmd.sunk | while | flops 202310912 | bytes 1846439 | solution.py:74
  342.0 1.5 broadcast_select_fusion.7
  345.5 1.5 broadcast_select_fusion.7
  362.5 1.5 broadcast_select_fusion.7
  365.9 1.5 broadcast_select_fusion.7
  369.3 1.5 broadcast_select_fusion.7
  382.9 1.5 broadcast_select_fusion.7
  385.1 42.2 %all-gather.19.cloned.1.call-done = f32[16,257,256]{2,1,0:T(8,128)} async-done(((f32[1,257,256]{2,1,0:T(8,128)}), f32[16,257,256]{2,1,0:T(8,128)}) %all-gather.19.cloned.1.call-update) | async-done | bytes 4210704 | tf_op jit(solution)/shard_map/all_gather | solution.py:13
  427.3 31.8 %while.110 = (s32[]{:T(128)}, f32[257,256]{1,0:T(8,128)S(1)}, s32[]{:T(128)}, f32[16,257,256]{2,1,0:T(8,128)}, s32[]{:T(128)}, /*index=5*/s32[]{:T(128)}, s32[]{:T(128)}, s32[]{:T(128)}, s32[]{}) while((s32[]{:T(128)}, f32[257,256]{1,0:T(8,128)S(1)}, s32[]{:T(128)}, f32[16,257,256]{2,1,0:T(8,128)}, s32[]{:T(128)}, /*index=5*/s32[]{:T(128)}, ...), condition=%wide.region_13.14_spmd, body=%wide.region_12.13_spmd.sunk | while | flops 202245120 | bytes 1320107 | solution.py:20
  459.6 6.3 %while.111 = (s32[]{:T(128)}, f32[256]{0:T(256)S(1)}, f32[16,256]{1,0:T(8,128)S(1)}, f32[256,256]{1,0:T(8,128)S(1)}, f32[16,256]{1,0:T(8,128)S(1)}, /*index=5*/s32[]{:T(128)}, s32[]{:T(128)}, s32[]{:T(128)}) while((s32[]{:T(128)}, f32[256]{0:T(256)S(1)}, f32[16,256]{1,0:T(8,128)S(1)}, f32[256,256]{1,0:T(8,128)S(1)}, ...), condition=%wide.region_15.16_spmd, body=%wide.region_14.15_spmd.sunk | while | flops 786691 | bytes 271465 | solution.py:120
  (529 shorter events, 175.5 us)
Async XLA Ops:
  7.2 195.4 %copy-start = (f32[256]{0:T(256)S(1)}, f32[256]{0:T(256)}, u32[]{:S(2)}) copy-start(f32[256]{0:T(256)} %param.25) | copy-start | bytes 3076
  7.2 96.6 %all-gather.13.cloned.1.call-start = ((), (), s32[]{:S(2)}) async-start(), calls=%async_computation | async-start | bytes 4595712 | tf_op jit(solution)/shard_map/all_gather | solution.py:61
  42.7 0.7 copy-start.4
  43.4 159.2 %all-gather.15.cloned.1.call-start = ((), (), s32[]{:S(2)}) async-start(), calls=%async_computation.1 | async-start | bytes 4595712 | tf_op jit(solution)/shard_map/all_gather | solution.py:13
  103.8 56.7 %copy-start.1 = (f32[256,256]{1,0:T(8,128)S(1)}, f32[256,256]{1,0:T(8,128)}, u32[]{:S(2)}) copy-start(f32[256,256]{1,0:T(8,128)} %param.24) | copy-start | bytes 786436
  159.7 0.7 copy-start.2
  160.4 169.6 %all-gather.17.cloned.1.call-start = ((), (), s32[]{:S(2)}) async-start(), calls=%async_computation.2 | async-start | bytes 4595712 | tf_op jit(solution)/shard_map/all_gather | solution.py:61
  161.9 41.2 %copy-start.5 = (f32[256]{0:T(256)S(1)}, f32[256]{0:T(256)}, u32[]{:S(2)}) copy-start(f32[256]{0:T(256)} %get-tuple-element.1116) | copy-start | bytes 3076
  236.4 93.5 %copy-start.6 = (f32[16,256]{1,0:T(8,128)}, f32[16,256]{1,0:T(8,128)S(1)}, u32[]{:S(2)}) copy-start(f32[16,256]{1,0:T(8,128)S(1)} %get-tuple-element.497) | copy-start | bytes 49156
  243.3 184.0 %all-gather.19.cloned.1.call-start = ((), (), s32[]{:S(2)}) async-start(), calls=%async_computation.3 | async-start | bytes 4595712 | tf_op jit(solution)/shard_map/all_gather | solution.py:13
  384.4 0.7 copy-start.3
Sparse Core Ops, SparseCore 0:
  43.5 60.1 all-gather.12
  160.5 42.0 all-gather.14
  243.4 86.5 all-gather.16
  385.3 42.0 all-gather.18
where the time goes:
time: 479 us; the launch traced here: 473 us
  waiting for transfers between devices  229 us (48%)
  matrix products  121 us (25%)
  local copies, waits for them, and re-layouts  70.9 us (15%)
  loops' own time  23.3 us (5%)
  other arithmetic  14.7 us (3%)
  between operations  14.1 us (3%)
    all_gather x2, waiting for transfers between devices, incoming_state(): gathered = lax.all_gather(own_map[None], 'inner', axis=0, tiled=True)  147 us
    all_gather x2, waiting for transfers between devices, entering(): gathered = lax.all_gather(part, axis)  82.2 us
    dot_general x47, matrix products, compose(): product = jnp.dot(earlier, later[:state_width], precision=HIGHEST)  68 us
    slice x47, local copies, waits for them, and re-layouts, compose(): return product + last_row(state_width) * later[state_width][None, :]  33.1 us
    dot_general x16, matrix products, compose_forward(): lax.dot_general(packed, step_matrix, (((1,), (1,)), ((), ())), precision=...  21.9 us
    another operation x2, loops' own time, incoming_state(): lax.scan(absorb, (identity, identity), (gathered, jnp.arange(inner_count,...  20.8 us
    dot_general x16, matrix products, forward(): predicted = jnp.dot(step_matrix, state, precision=HIGHEST)  19.6 us
    dynamic_slice x32, local copies, waits for them, and re-layouts, incoming_state(): lax.scan(absorb, (identity, identity), (gathered, jnp.arange(inner_count,...  18.6 us
  transfers between devices with their start and end apart: 4, of which 4 were waited for; matrix products, arithmetic and copies ran while one was open for 0% of the time, Pallas kernels for 0%

commit v1 on v0

--- a/solution.py
+++ b/solution.py
@@ -58,7 +58,9 @@
     identity = identity_map(state_width)
     inner_count = lax.axis_size("inner")
     inner_here = lax.axis_index("inner")
-    gathered = lax.all_gather(own_map[None], "inner", axis=0, tiled=True)
+    x = own_map[None]
+    sent = jnp.stack([x] * lax.axis_size("inner"))
+    gathered = jnp.concatenate(lax.all_to_all(sent, "inner", 0, 0), axis=0)
 
     def absorb(running, inputs):
         before, group_total = running

time: 479 us -> 527 us (1.10)
  local copies, waits for them, and re-layouts: 70.9 us -> 87.8 us
  waiting for transfers between devices: 229 us -> 245 us
  starting transfers between devices: 0.16 us -> 14.8 us
    all_gather x2 -> x0, waiting for transfers between devices: 147 us -> none  [incoming_state(): gathered = lax.all_gather(own_map[None], 'inner', axis=0, tiled=True)]
    all_to_all x0 -> x2, waiting for transfers between devices: none -> 109 us  [incoming_state(): gathered = jnp.concatenate(lax.all_to_all(sent, 'inner', 0, 0), axis=0)]
    all_gather x2, waiting for transfers between devices: 82.2 us -> 136 us  [entering(): gathered = lax.all_gather(part, axis)]
    all_to_all x0 -> x2, starting transfers between devices: none -> 14.8 us  [incoming_state(): gathered = jnp.concatenate(lax.all_to_all(sent, 'inner', 0, 0), axis=0)]
    reshape x0 -> x2, local copies, waits for them, and re-layouts: none -> 9.29 us  [incoming_state(): gathered = jnp.concatenate(lax.all_to_all(sent, 'inner', 0, 0), axis=0)]
    another operation x3 -> x5, local copies, waits for them, and re-layouts: 0.06 us -> 8.3 us  [the longest x2 8.24 us: incoming_state(): sent = jnp.stack([x] * lax.axis_size('inner'))]
where the time goes in v1:
time: 527 us; the launch traced here: 520 us
  waiting for transfers between devices  245 us (46%)
  matrix products  121 us (23%)
  local copies, waits for them, and re-layouts  87.8 us (17%)
  loops' own time  23.3 us (4%)
  starting transfers between devices  14.8 us (3%)
  between operations  14.4 us (3%)
  other arithmetic  14.1 us (3%)
    all_gather x2, waiting for transfers between devices, entering(): gathered = lax.all_gather(part, axis)  136 us
    all_to_all x2, waiting for transfers between devices, incoming_state(): gathered = jnp.concatenate(lax.all_to_all(sent, 'inner', 0, 0), axis=0)  109 us
    dot_general x47, matrix products, compose(): product = jnp.dot(earlier, later[:state_width], precision=HIGHEST)  68.2 us
    slice x47, local copies, waits for them, and re-layouts, compose(): return product + last_row(state_width) * later[state_width][None, :]  33.2 us
    dot_general x16, matrix products, compose_forward(): lax.dot_general(packed, step_matrix, (((1,), (1,)), ((), ())), precision=...  21.9 us
    another operation x2, loops' own time, incoming_state(): lax.scan(absorb, (identity, identity), (gathered, jnp.arange(inner_count,...  20.8 us
    dot_general x16, matrix products, forward(): predicted = jnp.dot(step_matrix, state, precision=HIGHEST)  19.6 us
    dynamic_slice x32, local copies, waits for them, and re-layouts, incoming_state(): lax.scan(absorb, (identity, identity), (gathered, jnp.arange(inner_count,...  18.6 us
  transfers between devices with their start and end apart: 4, of which 4 were waited for; matrix products, arithmetic and copies ran while one was open for 0% of the time, Pallas kernels for 0%

profile of v1, /device:TPU:2, one launch (start us, length us, event | category | flops | bytes accessed | tf_op | source)
XLA Modules:
  0.0 520.3 jit_solution(11222014332758654666)
XLA Ops:
  8.0 34.6 %while.112 = (s32[]{:T(128)}, f32[257,256]{1,0:T(8,128)S(1)}, f32[16,256,256]{2,1,0:T(8,128)}, f32[256]{0:T(256)S(1)}, f32[256]{0:T(256)}, /*index=5*/f32[16,256]{1,0:T(8,128)}, s32[]{:T(128)}) while((s32[]{:T(128)}, f32[257,256]{1,0:T(8,128)S(1)}, f32[16,256,256]{2,1,0:T(8,128)}, f32[256]{0:T(256)S(1)}, f32[256]{0:T(256)}, ...), condition=%wide.region_1.2_spmd.clone, body=%wide.region_0.1_spmd.clone.sunk | while | flops 202311168 | bytes 1322585 | solution.py:101
  42.6 4.1 stack.6
  46.8 7.5 %all-to-all-start = ((f32[16,1,257,256]{3,1,2,0:T(1,128)}), f32[16,1,257,256]{3,1,2,0:T(1,128)}, u32[]{:S(2)}, u32[]{:S(2)}) async-start(f32[16,1,257,256]{3,1,2,0:T(1,128)} %stack.6), calls=%async_computation | async-start | bytes 8421376 | tf_op jit(solution)/shard_map/all_to_all | solution.py:63
  54.4 54.3 %all-to-all-done = f32[16,1,257,256]{3,1,2,0:T(1,128)} async-done(((f32[16,1,257,256]{3,1,2,0:T(1,128)}), f32[16,1,257,256]{3,1,2,0:T(1,128)}, u32[]{:S(2)}, u32[]{:S(2)}) %all-to-all-start) | async-done | bytes 4210720 | tf_op jit(solution)/shard_map/all_to_all | solution.py:63
  108.7 4.6 copy.16
  113.3 56.0 %while.106 = (s32[]{:T(128)}, f32[257,256]{1,0:T(8,128)S(1)}, f32[257,256]{1,0:T(8,128)S(1)}, s32[16]{0:T(128)S(1)}, s32[]{:T(128)}, /*index=5*/f32[16,257,256]{2,1,0:T(8,128)}, s32[]{:T(128)}, s32[]{:T(128)}, s32[]{}) while((s32[]{:T(128)}, f32[257,256]{1,0:T(8,128)S(1)}, f32[257,256]{1,0:T(8,128)S(1)}, s32[16]{0:T(128)S(1)}, s32[]{:T(128)}, ...), condition=%wide.region_3.4_spmd, body=%wide.region_2.3_spmd.sunk | while | flops 202310912 | bytes 1846927 | solution.py:76
  115.4 1.5 broadcast_select_fusion.6
  125.9 1.5 broadcast_select_fusion.6
  136.3 1.5 broadcast_select_fusion.6
  157.3 1.5 broadcast_select_fusion.6
  172.2 54.8 %all-gather.7.cloned.1.call-done = f32[16,257,256]{2,1,0:T(8,128)} async-done(((f32[1,257,256]{2,1,0:T(8,128)}), f32[16,257,256]{2,1,0:T(8,128)}) %all-gather.7.cloned.1.call-update) | async-done | bytes 4210704 | tf_op jit(solution)/shard_map/all_gather | solution.py:13
  227.5 33.3 %while.108 = (s32[]{:T(128)}, f32[256]{0:T(256)S(1)}, f32[16,256]{1,0:T(8,128)S(1)}, f32[16,256]{1,0:T(8,128)S(1)}, f32[16,256,256]{2,1,0:T(8,128)}, /*index=5*/...) while((s32[]{:T(128)}, f32[256]{0:T(256)S(1)}, f32[16,256]{1,0:T(8,128)S(1)}, ...), condition=%wide.region_7.8_spmd, body=%wide.region_6.7_spmd.sunk | while | flops 787202 | bytes 275049 | solution.py:110
  260.9 6.1 %while.113 = (s32[]{:T(128)}, f32[256]{0:T(256)S(1)}, f32[256,256]{1,0:T(8,128)S(1)}, f32[16,256]{1,0:T(8,128)S(1)}, s32[]{:T(128)}, /*index=5*/s32[]{:T(128)}, s32[]{:T(128)}) while((s32[]{:T(128)}, f32[256]{0:T(256)S(1)}, f32[256,256]{1,0:T(8,128)S(1)}, f32[16,256]{1,0:T(8,128)S(1)}, s32[]{:T(128)}, /*index=5*/s32[]{:T(128)}, ...), condition=%wide.region_9.10_spmd.clone, body=%wide.region_8.9_spmd.clone.sunk | while | flops 786948 | bytes 271463 | solution.py:118
  267.0 4.1 stack.7
  271.1 7.3 %all-to-all-start.1 = ((f32[16,1,257,256]{3,1,2,0:T(1,128)}), f32[16,1,257,256]{3,1,2,0:T(1,128)}, u32[]{:S(2)}, u32[]{:S(2)}) async-start(f32[16,1,257,256]{3,1,2,0:T(1,128)} %stack.7), calls=%async_computation.1 | async-start | bytes 8421376 | tf_op jit(solution)/shard_map/all_to_all | solution.py:63
  278.5 54.2 %all-to-all-done.1 = f32[16,1,257,256]{3,1,2,0:T(1,128)} async-done(((f32[16,1,257,256]{3,1,2,0:T(1,128)}), f32[16,1,257,256]{3,1,2,0:T(1,128)}, u32[]{:S(2)}, u32[]{:S(2)}) %all-to-all-start.1) | async-done | bytes 4210720 | tf_op jit(solution)/shard_map/all_to_all | solution.py:63
  332.7 4.6 copy.15
  337.4 54.6 %while.109 = (s32[]{:T(128)}, f32[257,256]{1,0:T(8,128)S(1)}, f32[257,256]{1,0:T(8,128)S(1)}, s32[16]{0:T(128)S(1)}, s32[]{:T(128)}, /*index=5*/f32[16,257,256]{2,1,0:T(8,128)}, s32[]{:T(128)}, s32[]{:T(128)}, s32[]{:T(128)}, s32[]{}) while((s32[]{:T(128)}, f32[257,256]{1,0:T(8,128)S(1)}, f32[257,256]{1,0:T(8,128)S(1)}, s32[16]{0:T(128)S(1)}, ...), condition=%wide.region_11.12_spmd, body=%wide.region_10.11_spmd.sunk | while | flops 202310912 | bytes 1846439 | solution.py:76
  339.3 1.5 broadcast_select_fusion.7
  342.7 1.5 broadcast_select_fusion.7
  346.1 1.5 broadcast_select_fusion.7
  349.5 1.5 broadcast_select_fusion.7
  359.8 1.5 broadcast_select_fusion.7
  363.2 1.5 broadcast_select_fusion.7
  376.8 1.5 broadcast_select_fusion.7
  380.2 1.5 broadcast_select_fusion.7
  383.7 1.5 broadcast_select_fusion.7
  387.1 1.5 broadcast_select_fusion.7
  390.5 1.5 broadcast_select_fusion.7
  392.7 81.5 %all-gather.9.cloned.1.call-done = f32[16,257,256]{2,1,0:T(8,128)} async-done(((f32[1,257,256]{2,1,0:T(8,128)}), f32[16,257,256]{2,1,0:T(8,128)}) %all-gather.9.cloned.1.call-update) | async-done | bytes 4210704 | tf_op jit(solution)/shard_map/all_gather | solution.py:13
  474.2 31.8 %while.110 = (s32[]{:T(128)}, f32[257,256]{1,0:T(8,128)S(1)}, s32[]{:T(128)}, f32[16,257,256]{2,1,0:T(8,128)}, s32[]{:T(128)}, /*index=5*/s32[]{:T(128)}, s32[]{:T(128)}, s32[]{:T(128)}, s32[]{}) while((s32[]{:T(128)}, f32[257,256]{1,0:T(8,128)S(1)}, s32[]{:T(128)}, f32[16,257,256]{2,1,0:T(8,128)}, s32[]{:T(128)}, /*index=5*/s32[]{:T(128)}, ...), condition=%wide.region_13.14_spmd, body=%wide.region_12.13_spmd.sunk | while | flops 202245120 | bytes 1320107 | solution.py:20
  506.5 6.4 %while.111 = (s32[]{:T(128)}, f32[256]{0:T(256)S(1)}, f32[16,256]{1,0:T(8,128)S(1)}, f32[256,256]{1,0:T(8,128)S(1)}, f32[16,256]{1,0:T(8,128)S(1)}, /*index=5*/s32[]{:T(128)}, s32[]{:T(128)}, s32[]{:T(128)}) while((s32[]{:T(128)}, f32[256]{0:T(256)S(1)}, f32[16,256]{1,0:T(8,128)S(1)}, f32[256,256]{1,0:T(8,128)S(1)}, ...), condition=%wide.region_15.16_spmd, body=%wide.region_14.15_spmd.sunk | while | flops 786691 | bytes 271465 | solution.py:122
  (534 shorter events, 183.0 us)
Async XLA Ops:
  7.2 219.8 %copy-start = (f32[256]{0:T(256)S(1)}, f32[256]{0:T(256)}, u32[]{:S(2)}) copy-start(f32[256]{0:T(256)} %param.25) | copy-start | bytes 3076
  7.2 271.2 %copy-start.1 = (f32[257,256]{1,0:T(8,128)}, f32[257,256]{1,0:T(8,128)S(1)}, u32[]{:S(2)}) copy-start(f32[257,256]{1,0:T(8,128)S(1)} %pad_convert_fusion) | copy-start | bytes 789508
  46.8 61.9 %all-to-all-start = ((f32[16,1,257,256]{3,1,2,0:T(1,128)}), f32[16,1,257,256]{3,1,2,0:T(1,128)}, u32[]{:S(2)}, u32[]{:S(2)}) async-start(f32[16,1,257,256]{3,1,2,0:T(1,128)} %stack.6), calls=%async_computation | async-start | bytes 8421376 | tf_op jit(solution)/shard_map/all_to_all | solution.py:63
  54.2 172.8 %all-gather.7.cloned.1.call-start = ((), (), s32[]{:S(2)}) async-start(), calls=%async_computation.2 | async-start | bytes 4595712 | tf_op jit(solution)/shard_map/all_gather | solution.py:13
  113.3 56.8 %copy-start.5 = (f32[256,256]{1,0:T(8,128)S(1)}, f32[256,256]{1,0:T(8,128)}, u32[]{:S(2)}) copy-start(f32[256,256]{1,0:T(8,128)} %param.24) | copy-start | bytes 786436
  169.3 0.7 copy-start.6
  171.5 56.0 %copy-start.7 = (f32[256]{0:T(256)S(1)}, f32[256]{0:T(256)}, u32[]{:S(2)}) copy-start(f32[256]{0:T(256)} %get-tuple-element.1124) | copy-start | bytes 3076
  260.8 10.2 %copy-start.8 = (f32[16,256]{1,0:T(8,128)}, f32[16,256]{1,0:T(8,128)S(1)}, u32[]{:S(2)}) copy-start(f32[16,256]{1,0:T(8,128)S(1)} %get-tuple-element.497) | copy-start | bytes 49156
  271.1 61.6 %all-to-all-start.1 = ((f32[16,1,257,256]{3,1,2,0:T(1,128)}), f32[16,1,257,256]{3,1,2,0:T(1,128)}, u32[]{:S(2)}, u32[]{:S(2)}) async-start(f32[16,1,257,256]{3,1,2,0:T(1,128)} %stack.7), calls=%async_computation.1 | async-start | bytes 8421376 | tf_op jit(solution)/shard_map/all_to_all | solution.py:63
  278.4 195.9 %all-gather.9.cloned.1.call-start = ((), (), s32[]{:S(2)}) async-start(), calls=%async_computation.3 | async-start | bytes 4595712 | tf_op jit(solution)/shard_map/all_gather | solution.py:13
  278.4 58.9 %copy-start.4 = (f32[257,256]{1,0:T(8,128)S(1)}, f32[257,256]{1,0:T(8,128)}, u32[]{:S(2)}) copy-start(f32[257,256]{1,0:T(8,128)} %copy-done.1) | copy-start | bytes 789508
  337.3 136.9 %copy-start.2 = (f32[257,256]{1,0:T(8,128)S(1)}, f32[257,256]{1,0:T(8,128)}, u32[]{:S(2)}) copy-start(f32[257,256]{1,0:T(8,128)} %copy-done.1) | copy-start | bytes 789508
  392.0 0.7 copy-start.3
Sparse Core Ops, SparseCore 0:
  170.2 56.7 all-gather.6
  392.8 81.3 all-gather.8
